TPU v7x, 32 devices: a whole 2x2x4 slice. The times are simulated.
32 devices in a mesh: lat: 8 (over z, y), lon: 4 (over x, core).
Axes of the slice: x: 2, y: 2, z: 4, core: 2. Of those that a mesh axis runs over, the one named last changes fastest.
Arguments:
- fields: bfloat16 [69, 128, 512], P(None, 'lat', 'lon'), may hold values from -6 to 6
- enc_kernel: bfloat16 [3, 3, 256, 69], replicated, may hold values from -0.25 to 0.25
- gen_kernel: bfloat16 [3, 3, 69, 256], replicated, may hold values from -0.125 to 0.125
- recon_grad: bfloat16 [69, 128, 512], P(None, 'lat', 'lon'), may hold values from -6 to 6
Outputs:
- rebuilt: bfloat16 [69, 128, 512], P(None, 'lat', 'lon')
- feat_grad: bfloat16 [256, 128, 512], P(None, 'lat', 'lon')
- enc_grad: float32 [3, 3, 256, 69], replicated
- gen_grad: float32 [3, 3, 69, 256], replicated
All inputs are finite; a program needn't handle non-finite values.
Results may differ from a plain program's by a relative error of at most 0.0085.
Values may be sent and summed in bfloat16 or wider, within the bound.
A program may use at most 64 MiB of HBM per device.

v0:
```python
import functools

import jax
import jax.numpy as jnp
from jax import lax
from jax.experimental import pallas as pl
from jax.experimental.pallas import tpu as pltpu
from jax.sharding import PartitionSpec as P

MESH = pl.DeviceIdType.MESH
LINK = jnp.bfloat16
F32 = jnp.float32
BF16 = jnp.bfloat16


def dot(left, right, dims):
    return lax.dot_general(left, right, (dims, ((), ())), preferred_element_type=F32)


def shifted(value, amount):
    width = value.shape[1]
    if isinstance(amount, int):
        amount = amount % width
        if amount == 0:
            return value
    return pltpu.roll(value, amount, 1)


def layer_kernel(
    lats, halves, deep, f_hbm, g_hbm, we_hbm, wg_hbm, reb_ref, feat_ref, grad_ref,
    fin, win, flat, xg, colp, colh, corner, hrow, dact, feat_rows, wpad, we, wf, wr,
    ysum, ycol, yhalo, turned, accx, accg, parts, from_pair, lon_out, from_lon, lat_out, from_lat,
    local_sem, *sems,
):
    count, height, width = fin.shape[1:]
    hid = hrow.shape[1]
    lons = 2 * halves
    band = 3 * deep
    half_deep = deep // 2
    lat = lax.axis_index("lat")
    lon = lax.axis_index("lon")
    half = lax.div(lon, 2)
    core = lax.rem(lon, 2)
    other = 1 - core
    below_top = lax.div(lat + lats - 1, lats)
    above_end = lax.div(2 * lats - 2 - lat, lats)

    def lon_peer(step):
        return (lat, lax.rem(half + step, halves) * 2 + core)

    def lat_peer(step):
        return (lax.rem(lat + step, lats), lon)

    def north_of(place):
        return (lat - below_top, lax.rem(place + (1 - below_top) * halves, lons))

    def south_of(place):
        return (lat + above_end, lax.rem(place + (1 - above_end) * halves, lons))

    west_lon = lax.rem(lon + lons - 1, lons)
    east_lon = lax.rem(lon + 1, lons)
    pair = (lat, half * 2 + other)
    west = (lat, west_lon)
    east = (lat, east_lon)
    north = north_of(lon)
    south = south_of(lon)
    diagonals = [
        (south_of(east_lon), 1 - above_end, 0),
        (north_of(east_lon), below_top, 0),
        (south_of(west_lon), 1 - above_end, 1),
        (north_of(west_lon), below_top, 1),
    ]

    barrier = pltpu.get_barrier_semaphore()
    peers = [west, east] + [peer for peer, slot, side in diagonals]
    peers += [lon_peer(step) for step in range(1, halves)]
    peers += [lat_peer(step) for step in range(1, lats)]
    for peer in peers:
        pl.semaphore_signal(barrier, inc=1, device_id=peer, device_id_type=MESH)

    loads = [
        pltpu.make_async_copy(f_hbm, fin.at[0], local_sem.at[0]),
        pltpu.make_async_copy(g_hbm, fin.at[1], local_sem.at[1]),
        pltpu.make_async_copy(we_hbm, win.at[0], local_sem.at[2]),
        pltpu.make_async_copy(wg_hbm, win.at[1], local_sem.at[3]),
    ]
    for load in loads:
        load.start()

    def send(src, dst, phase, send_slot, recv_slot, peer):
        copy = pltpu.make_async_remote_copy(
            src_ref=src,
            dst_ref=dst,
            send_sem=sems[2 * phase].at[send_slot],
            recv_sem=sems[2 * phase + 1].at[recv_slot],
            device_id=peer,
            device_id_type=MESH,
        )
        copy.start()
        return copy

    def arrive(ref, phase, slot):
        pltpu.make_async_copy(ref, ref, sems[2 * phase + 1].at[slot]).wait()

    lane = lax.broadcasted_iota(jnp.int32, (deep, width), 1)
    half_lane = lax.broadcasted_iota(jnp.int32, (half_deep, width), 1)
    rim = (lane == 0) | (lane == width - 1)

    for array in range(2):
        flat[array, count * height :] = jnp.zeros(((deep - count) * height, width), F32)
        wpad[array, :, deep - 16 :] = jnp.zeros((9, 16, hid), BF16)
    accx[...] = jnp.zeros_like(accx)
    accg[...] = jnp.zeros_like(accg)
    for load in loads[:2]:
        load.wait()
    for array in range(2):
        flat[array, : count * height] = fin[array].astype(F32).reshape(count * height, width)

    def cells_of(array, row):
        return flat[array, pl.ds(row, deep, stride=height), :]

    packed = jnp.zeros((half_deep, width), F32)
    for row in range(height):
        for array in range(2):
            cells = cells_of(array, row)
            xg[row + 1, array * band + deep : array * band + 2 * deep] = cells.astype(BF16)
            rims = jnp.where(rim, cells, 0.0)
            for part in range(2):
                packed = packed + shifted(
                    rims[part * half_deep : (part + 1) * half_deep],
                    2 * row + 1 + (2 * array + part) * 2 * height,
                )
    colp[...] = packed.astype(BF16)

    pl.semaphore_wait(barrier, len(peers))
    col_copies = [
        send(colp, colh.at[0], 12, 0, 0, east),
        send(colp, colh.at[1], 12, 1, 1, west),
    ]

    def send_rows(array):
        middle = pl.ds(array * band + deep, deep)
        return [
            send(
                xg.at[1, middle], xg.at[below_top * (height + 1), middle],
                13, 2 * array, 2 * array + below_top, north,
            ),
            send(
                xg.at[height, middle], xg.at[(1 - above_end) * (height + 1), middle],
                13, 2 * array + 1, 2 * array + 1 - above_end, south,
            ),
        ]

    row_copies = send_rows(0)
    corner_copies = [
        send(colp, corner.at[slot, side], 14, index, 2 * slot + side, peer)
        for index, (peer, slot, side) in enumerate(diagonals)
    ]
    row_copies += send_rows(1)

    for load in loads[2:]:
        load.wait()
    for array in range(2):
        for tap in range(9):
            row_tap, col_tap = divmod(tap, 3)
            target = (2 - row_tap) * 3 + col_tap if array else tap
            wpad[array, target, :count] = win[array, tap]
    for tap in range(9):
        row_tap, col_tap = divmod(tap, 3)
        wr[col_tap * deep : (col_tap + 1) * deep, row_tap * hid : (row_tap + 1) * hid] = wpad[
            1, (2 - row_tap) * 3 + col_tap
        ]
    line = lax.broadcasted_iota(jnp.int32, (hid, hid), 0)
    column = lax.broadcasted_iota(jnp.int32, (hid, hid), 1)
    eye = jnp.where(line == column, 1.0, 0.0).astype(BF16)
    for array, target in ((0, we), (1, wf)):
        target[...] = dot(eye, wpad[array].reshape(9 * deep, hid), ((1,), (1,))).astype(BF16)

    even = lax.rem(half_lane, 2) == 0

    def join(from_west, from_east):
        return jnp.where(
            even, shifted(from_east.astype(F32), -1), shifted(from_west.astype(F32), 1)
        )

    def widen(array, slot, cells, rims, turn):
        parts_in = []
        for part in range(2):
            group = (2 * array + part) * 2 * height
            parts_in.append(shifted(rims, turn(group)))
        edges = jnp.concatenate(parts_in, axis=0)
        before = jnp.where(lane == 0, edges, shifted(cells, 1)).astype(BF16)
        after = jnp.where(lane == width - 1, edges, shifted(cells, -1)).astype(BF16)
        first, last = (after, before) if array else (before, after)
        base = array * band
        xg[slot, base : base + deep] = first
        xg[slot, base + 2 * deep : base + band] = last

    for copy in col_copies:
        copy.wait()
    own_rims = join(colh[0], colh[1])

    def widen_own(array):
        for row in range(height):
            widen(
                array, row + 1, cells_of(array, row), own_rims,
                lambda group: -(2 * row + 1 + group),
            )

    widen_own(0)
    for copy in corner_copies:
        copy.wait_send()
    for slot in range(4):
        arrive(corner.at[slot // 2, slot % 2], 14, slot)
    for copy in row_copies:
        copy.wait_send()
    halo_rims = [join(corner[slot, 0], corner[slot, 1]) for slot in range(2)]
    source_rows = (below_top * (height - 1), (1 - above_end) * (height - 1))

    def widen_halo(array):
        middle = pl.ds(array * band + deep, deep)
        for slot in range(2):
            arrive(xg.at[slot * (height + 1), middle], 13, 2 * array + slot)
        for slot in range(2):
            cells = xg[slot * (height + 1), array * band + deep : array * band + 2 * deep]
            at = source_rows[slot]
            widen(
                array, slot * (height + 1), cells.astype(F32), halo_rims[slot],
                lambda group: lax.rem(2 * width - (2 * at + 1 + group), width),
            )

    widen_halo(0)
    widen_own(1)
    widen_halo(1)

    ends = ((0, below_top, 2 * band, 0), (1, above_end, 0, height - 1))
    at_poles = []
    for slot, inside, start, row in ends:
        edge = xg[slot * (height + 1), band:]
        at_poles.append(jnp.where(inside == 0, edge, jnp.zeros_like(edge)))
        xg[slot * (height + 1), band:] = jnp.where(inside == 0, jnp.zeros_like(edge), edge)

    rows = 4
    steps = height // rows

    def window(ref, row, start, size):
        return jnp.concatenate(
            [
                ref[pl.ds(row + place, 3), start : start + size].reshape(3 * size, width)
                for place in range(rows)
            ],
            axis=1,
        )

    def first_step(step):
        row = step * rows
        pre_act = dot(we[...], window(xg, row, 0, band), ((1,), (0,)))
        logistic = 1.0 / (1.0 + jnp.exp(-pre_act))
        gated = pre_act * logistic
        dact[step] = logistic + gated * (1.0 - logistic)
        hidden = gated.astype(BF16)
        for place in range(rows):
            hrow[row + 1 + place] = hidden[:, place * width : (place + 1) * width]
        accg[...] += dot(window(xg, row, band, band), hidden, ((1,), (1,)))

    def second_step(step, extra):
        row = step * rows
        feat = dot(wf[...], window(xg, row, band, band), ((1,), (0,)))
        if extra is not None:
            feat = feat + extra
        feat = feat.astype(BF16)
        for place in range(rows):
            feat_rows[row + place] = feat[:, place * width : (place + 1) * width]
        pre_grad = (feat.astype(F32) * dact[step]).astype(BF16)
        accx[...] += dot(window(xg, row, 0, band), pre_grad, ((1,), (1,)))

    for step in range(steps):
        first_step(step)
    hid_copies = [
        send(hrow.at[1], hrow.at[below_top * (height + 1)], 15, 0, below_top, north),
        send(hrow.at[height], hrow.at[(1 - above_end) * (height + 1)], 15, 1, 1 - above_end, south),
    ]
    for slot, inside, start, row in ends:
        accg[start : start + band] += dot(at_poles[slot], hrow[row + 1], ((1,), (1,)))

    side_lanes = hid // 2
    per = lon_out.shape[2]

    def fill(stream, acc, backward):
        used = 9 * count
        for tap in range(9):
            row_tap, col_tap = divmod(tap, 3)
            source = ((2 - row_tap) * 3 + col_tap if backward else tap) * deep
            for side in range(2):
                parts[stream, side, tap * count : (tap + 1) * count] = acc[
                    source : source + count, side * side_lanes : (side + 1) * side_lanes
                ]
        spare = parts.shape[2] - used
        if spare:
            for side in range(2):
                parts[stream, side, used:] = jnp.zeros((spare, side_lanes), F32)

    def piece(index, size):
        return pl.ds(pl.multiple_of(index * size, 8), size)

    order = sorted(range(1, lats), key=lambda step: abs(2 * step - lats))

    def start_pair(stream):
        copies = {}
        for step in list(range(1, halves)) + [0]:
            part = piece(lax.rem(half + step, halves), lats * per)
            copies[step] = send(
                parts.at[stream, other, part], from_pair.at[stream, part], stream * 6, step, step, pair
            )
        return copies

    def start_lon(stream, copies):
        onward = {}
        for step in range(1, halves):
            copies[step].wait()
            target = lax.rem(half + step, halves)
            for turn in order + [0]:
                there = lax.rem(lat + turn, lats)
                chunk = target * lats + there
                part = piece(chunk, per)
                lon_out[stream, chunk] = (
                    parts[stream, core, part] + from_pair[stream, part]
                ).astype(LINK)
                onward[step, turn] = send(
                    lon_out.at[stream, chunk],
                    from_lon.at[stream, step - 1, there],
                    stream * 6 + 1, (step - 1) * lats + turn, (step - 1) * lats + turn, lon_peer(step),
                )
        copies[0].wait()
        return onward

    def lon_total(stream, copies, turn):
        there = lax.rem(lat + turn, lats)
        part = piece(half * lats + there, per)
        total = parts[stream, core, part] + from_pair[stream, part]
        for step in range(1, halves):
            copies[step, turn].wait()
            total = total + from_lon[stream, step - 1, there].astype(F32)
        return total

    def start_lat(stream, copies):
        onward = []
        for turn in order:
            there = lax.rem(lat + turn, lats)
            lat_out[stream, there] = lon_total(stream, copies, turn).astype(LINK)
            onward.append(
                send(
                    lat_out.at[stream, there], from_lat.at[stream, turn - 1],
                    stream * 6 + 2, turn - 1, turn - 1, lat_peer(turn),
                )
            )
        return onward, lon_total(stream, copies, 0)

    def spread(stream, turn, lon_copies, pair_copies):
        there = lax.rem(lat + lats - turn, lats)
        mine = grad_ref.at[stream, core, half * lats + there]
        for step in range(1, halves):
            slot = (step - 1) * lats + turn
            lon_copies[step, turn] = send(mine, mine, stream * 6 + 4, slot, slot, lon_peer(step))
        pair_copies.append(send(mine, mine, stream * 6 + 5, turn, turn, pair))

    def start_lat_gather(stream, started):
        copies, total = started
        for turn, copy in zip(order, copies):
            copy.wait()
            total = total + from_lat[stream, turn - 1].astype(F32)
        place = half * lats + lat
        grad_ref[stream, core, place] = total.astype(grad_ref.dtype)
        mine = grad_ref.at[stream, core, place]
        copies = [
            send(mine, mine, stream * 6 + 3, turn - 1, turn - 1, lat_peer(turn)) for turn in order
        ]
        lon_copies, pair_copies = {}, []
        spread(stream, 0, lon_copies, pair_copies)
        return copies, lon_copies, pair_copies

    def start_spread(stream, started):
        copies, lon_copies, pair_copies = started
        for turn, copy in reversed(list(zip(order, copies))):
            copy.wait()
            spread(stream, turn, lon_copies, pair_copies)
        return lon_copies, pair_copies

    def start_pair_gather(stream, started):
        lon_copies, pair_copies = started
        for turn in [0] + order[::-1]:
            for step in range(1, halves):
                lon_copies[step, turn].wait()
                source = lax.rem(half + halves - step, halves)
                there = lax.rem(lat + lats - turn, lats)
                mine = grad_ref.at[stream, core, source * lats + there]
                slot = step * lats + turn
                pair_copies.append(send(mine, mine, stream * 6 + 5, slot, slot, pair))
        return pair_copies

    def pole_term(slot, start):
        return dot(wf[:, start : start + band], at_poles[slot], ((1,), (0,)))

    fill(0, accg, True)
    gen_copies = start_pair(0)
    open_gap = jnp.zeros((hid, (rows - 1) * width), F32)
    for step in range(steps):
        extra = None
        if step == 0:
            extra = jnp.concatenate([pole_term(0, 2 * band), open_gap], axis=1)
        elif step == steps - 1:
            extra = jnp.concatenate([open_gap, pole_term(1, 0)], axis=1)
        second_step(step, extra)
        if step == 1:
            gen_copies = start_lon(0, gen_copies)
    fill(1, accx, False)
    enc_copies = start_pair(1)

    for copy in hid_copies:
        copy.wait_send()
    for slot in range(2):
        arrive(hrow.at[slot * (height + 1)], 15, slot)

    def rebuild_step(step, packed):
        value = dot(wr[...], window(hrow, step * rows, 0, hid), ((1,), (0,)))
        for place in range(rows):
            row = step * rows + place
            lanes = slice(place * width, (place + 1) * width)
            left, centre, right = (value[tap * deep : (tap + 1) * deep, lanes] for tap in range(3))
            packed = packed + shifted(
                jnp.where(lane == width - 1, left, jnp.where(lane == 0, right, 0.0)), 2 * row + 1
            )
            inner = jnp.where(lane == 0, 0.0, shifted(left, 1))
            inner = inner + centre
            inner = inner + jnp.where(lane == width - 1, 0.0, shifted(right, -1))
            ysum[row] = inner
        return packed

    packed = jnp.zeros((deep, width), F32)
    packed = rebuild_step(0, packed)
    enc_copies = start_lon(1, enc_copies)
    gen_copies = start_lat(0, gen_copies)
    for step in range(1, steps):
        packed = rebuild_step(step, packed)
    ycol[...] = packed
    y_copies = [
        send(ycol, yhalo.at[0], 16, 0, 0, east),
        send(ycol, yhalo.at[1], 16, 1, 1, west),
    ]
    enc_copies = start_lat(1, enc_copies)

    def turn_out(load, target, size):
        for row in range(height):
            turned[pl.ds(row, size, stride=height), :] = load(row)
        target[...] = turned[: target.shape[0] * height].reshape(target.shape).astype(BF16)

    turn_out(lambda row: feat_rows[row].astype(F32), feat_ref, hid)
    gen_copies = start_lat_gather(0, gen_copies)
    for copy in y_copies:
        copy.wait()
    y_rims = jnp.where(lax.rem(lane, 2) == 0, shifted(yhalo[1], -1), shifted(yhalo[0], 1))

    def rebuilt_row(row):
        edges = shifted(y_rims, -(2 * row + 1))
        return ysum[row] + jnp.where((lane == 0) | (lane == width - 1), edges, 0.0)

    turn_out(rebuilt_row, reb_ref, deep)
    enc_copies = start_lat_gather(1, enc_copies)
    gen_copies = start_spread(0, gen_copies)
    gen_copies = start_pair_gather(0, gen_copies)
    enc_copies = start_spread(1, enc_copies)
    enc_copies = start_pair_gather(1, enc_copies)
    for copy in gen_copies + enc_copies:
        copy.wait()


def finish_kernel(norm, reb_in, feat_in, grad_in, reb_out, feat_out, enc_out, gen_out, flat, ready, sem):
    taps, count, hid = enc_out.shape
    side_lanes = hid // 2
    copies = [
        pltpu.make_async_copy(feat_in, feat_out, sem.at[0]),
        pltpu.make_async_copy(reb_in, reb_out, sem.at[1]),
    ]
    for copy in copies:
        copy.start()
    for stream, out in ((0, gen_out), (1, enc_out)):
        for side in range(2):
            gathered = grad_in[stream, side].astype(F32) * norm
            flat[:, side * side_lanes : (side + 1) * side_lanes] = gathered.reshape(-1, side_lanes)
        for tap in range(taps):
            ready[stream, tap] = flat[tap * count : (tap + 1) * count]
        copies.append(pltpu.make_async_copy(ready.at[stream], out, sem.at[2 + stream]))
        copies[-1].start()
    for copy in copies:
        copy.wait()


def on_device(fields, enc_kernel, gen_kernel, recon_grad):
    count, height, width = fields.shape
    hid = enc_kernel.shape[2]
    deep = -(-count // 16) * 16
    lats = lax.axis_size("lat")
    lons = lax.axis_size("lon")
    halves = lons // 2
    band = 3 * deep
    side_lanes = hid // 2
    chunks = halves * lats
    per = -(-9 * count // (chunks * 8)) * 8
    hops = (halves - 1) * lats
    counts = [halves, hops, lats - 1, lats - 1, hops, chunks] * 2 + [2, 4, 4, 2, 2]
    vmem = pl.BlockSpec(memory_space=pltpu.VMEM)
    anywhere = pl.BlockSpec(memory_space=pltpu.HBM)
    rebuilt, feat, summed = pl.pallas_call(
        functools.partial(layer_kernel, lats, halves, deep),
        out_shape=[
            jax.ShapeDtypeStruct((count, height, width), BF16),
            jax.ShapeDtypeStruct((hid, height, width), BF16),
            jax.ShapeDtypeStruct((2, 2, chunks, per, side_lanes), BF16),
        ],
        in_specs=[anywhere] * 4,
        out_specs=[vmem] * 3,
        scratch_shapes=[
            pltpu.VMEM((2, count, height, width), BF16),
            pltpu.VMEM((2, 9, count, hid), BF16),
            pltpu.VMEM((2, deep * height, width), F32),
            pltpu.VMEM((height + 2, 2 * band, width), BF16),
            pltpu.VMEM((deep // 2, width), BF16),
            pltpu.VMEM((2, deep // 2, width), BF16),
            pltpu.VMEM((2, 2, deep // 2, width), BF16),
            pltpu.VMEM((height + 2, hid, width), BF16),
            pltpu.VMEM((height // 4, hid, 4 * width), F32),
            pltpu.VMEM((height, hid, width), BF16),
            pltpu.VMEM((2, 9, deep, hid), BF16),
            pltpu.VMEM((hid, 9 * deep), BF16),
            pltpu.VMEM((hid, 9 * deep), BF16),
            pltpu.VMEM((band, 3 * hid), BF16),
            pltpu.VMEM((height, deep, width), F32),
            pltpu.VMEM((deep, width), F32),
            pltpu.VMEM((2, deep, width), F32),
            pltpu.VMEM((hid * height, width), F32),
            pltpu.VMEM((9 * deep, hid), F32),
            pltpu.VMEM((9 * deep, hid), F32),
            pltpu.VMEM((2, 2, chunks * per, side_lanes), F32),
            pltpu.VMEM((2, chunks * per, side_lanes), F32),
            pltpu.VMEM((2, chunks, per, side_lanes), LINK),
            pltpu.VMEM((2, halves - 1, lats, per, side_lanes), LINK),
            pltpu.VMEM((2, lats, per, side_lanes), LINK),
            pltpu.VMEM((2, lats - 1, per, side_lanes), LINK),
            pltpu.SemaphoreType.DMA((4,)),
        ]
        + [pltpu.SemaphoreType.DMA((size,)) for size in counts for _ in range(2)],
        compiler_params=pltpu.CompilerParams(
            collective_id=0, has_side_effects=True, vmem_limit_bytes=48 << 20
        ),
    )(
        fields,
        recon_grad,
        enc_kernel.transpose(0, 1, 3, 2).reshape(9, count, hid),
        gen_kernel.reshape(9, count, hid),
    )
    norm = 1.0 / float(height * lats * width * lons) ** 0.5
    rebuilt, feat, enc_grad, gen_grad = pl.pallas_call(
        functools.partial(finish_kernel, norm),
        out_shape=[
            jax.ShapeDtypeStruct((count, height, width), BF16),
            jax.ShapeDtypeStruct((hid, height, width), BF16),
            jax.ShapeDtypeStruct((9, count, hid), F32),
            jax.ShapeDtypeStruct((9, count, hid), F32),
        ],
        in_specs=[vmem] * 3,
        out_specs=[anywhere] * 4,
        scratch_shapes=[
            pltpu.VMEM((chunks * per, hid), F32),
            pltpu.VMEM((2, 9, count, hid), F32),
            pltpu.SemaphoreType.DMA((4,)),
        ],
    )(rebuilt, feat, summed)
    return (
        rebuilt,
        feat,
        enc_grad.reshape(3, 3, count, hid).transpose(0, 1, 3, 2),
        gen_grad.reshape(3, 3, count, hid),
    )


def solution(mesh):
    return jax.shard_map(
        on_device,
        mesh=mesh,
        in_specs=(P(None, "lat", "lon"), P(), P(), P(None, "lat", "lon")),
        out_specs=(P(None, "lat", "lon"), P(None, "lat", "lon"), P(), P()),
        check_vma=False,
    )
```

profile of v0, /device:TPU:0, one launch (start us, length us, event | category | flops | bytes accessed | tf_op | source)
XLA Modules:
  0.0 46.4 jit_solution(3191501201277189767)
XLA Ops:
  0.6 0.0 copy-start.2
  0.6 1.0 %copy-done.2 = bf16[3,3,256,69]{2,3,1,0:T(8,128)(2,1)S(1)} copy-done((bf16[3,3,256,69]{2,3,1,0:T(8,128)(2,1)S(1)}, bf16[3,3,256,69]{2,3,1,0:T(8,128)(2,1)}, u32[]{:S(2)}) %copy-start.2) | copy-done | bytes 317976
  1.6 0.0 copy-start.3
  1.6 1.0 %copy-done.3 = bf16[3,3,69,256]{3,2,1,0:T(8,128)(2,1)S(1)} copy-done((bf16[3,3,69,256]{3,2,1,0:T(8,128)(2,1)S(1)}, bf16[3,3,69,256]{3,2,1,0:T(8,128)(2,1)}, u32[]{:S(2)}) %copy-start.3) | copy-done | bytes 317976
  2.6 0.0 copy-start.4
  2.6 1.0 %copy-done.4 = bf16[69,16,128]{2,1,0:T(8,128)(2,1)S(1)} copy-done((bf16[69,16,128]{2,1,0:T(8,128)(2,1)S(1)}, bf16[69,16,128]{2,1,0:T(8,128)(2,1)}, u32[]{:S(2)}) %copy-start.4) | copy-done | bytes 282648
  3.5 0.0 copy-start.5
  3.5 1.0 %copy-done.5 = bf16[69,16,128]{2,1,0:T(8,128)(2,1)S(1)} copy-done((bf16[69,16,128]{2,1,0:T(8,128)(2,1)S(1)}, bf16[69,16,128]{2,1,0:T(8,128)(2,1)}, u32[]{:S(2)}) %copy-start.5) | copy-done | bytes 282648
  4.5 36.3 %shard_map.75 = (bf16[69,16,128]{2,1,0:T(8,128)(2,1)S(1)}, bf16[256,16,128]{2,1,0:T(8,128)(2,1)S(1)}, bf16[2,2,16,40,128]{4,3,2,1,0:T(8,128)(2,1)S(1)}) custom-call(bf16[69,16,128]{2,1,0:T(8,128)(2,1)S(1)} %copy-done.4, bf16[69,16,128]{2,1,0:T(8,128)(2,1)S(1)} %copy-done.5, bf16[9,69,256]{2,1,0:T(8,128)(2,1)S(1)} %bitcast.8, bf16[9,69,256]{2,1,0:T(8,128)(2,1)S(1)} %bitcast.9), custom_call_target="tpu_custom_call" | custom-call | tf_op jit(solution)/shard_map/pallas_call | solution.py:513
  40.8 0.0 copy-start
  40.8 1.0 %copy-done = bf16[256,16,128]{2,1,0:T(8,128)(2,1)} copy-done((bf16[256,16,128]{2,1,0:T(8,128)(2,1)}, bf16[256,16,128]{2,1,0:T(8,128)(2,1)S(1)}, u32[]{:S(2)}) %copy-start) | copy-done | bytes 1048600
  41.8 0.0 copy-start.1
  41.8 0.9 %copy-done.1 = bf16[2,2,16,40,128]{4,3,2,1,0:T(8,128)(2,1)} copy-done((bf16[2,2,16,40,128]{4,3,2,1,0:T(8,128)(2,1)}, bf16[2,2,16,40,128]{4,3,2,1,0:T(8,128)(2,1)S(1)}, u32[]{:S(2)}) %copy-start.1) | copy-done | bytes 655384
  42.7 0.0 copy-start.6
  42.7 0.7 %copy-done.6 = bf16[69,16,128]{2,1,0:T(8,128)(2,1)} copy-done((bf16[69,16,128]{2,1,0:T(8,128)(2,1)}, bf16[69,16,128]{2,1,0:T(8,128)(2,1)S(1)}, u32[]{:S(2)}) %copy-start.6) | copy-done | bytes 282648
  43.4 3.0 %shard_map.76 = (bf16[69,16,128]{2,1,0:T(8,128)(2,1)}, bf16[256,16,128]{2,1,0:T(8,128)(2,1)}, f32[9,69,256]{2,1,0:T(8,128)}, f32[9,69,256]{2,1,0:T(8,128)}) custom-call(bf16[69,16,128]{2,1,0:T(8,128)(2,1)} %copy-done.6, bf16[256,16,128]{2,1,0:T(8,128)(2,1)} %copy-done, bf16[2,2,16,40,128]{4,3,2,1,0:T(8,128)(2,1)} %copy-done.1), custom_call_target="tpu_custom_call" | custom-call | tf_op jit(solution)/shard_map/pallas_call | solution.py:562
Async XLA Ops:
  0.6 1.0 %copy-start.2 = (bf16[3,3,256,69]{2,3,1,0:T(8,128)(2,1)S(1)}, bf16[3,3,256,69]{2,3,1,0:T(8,128)(2,1)}, u32[]{:S(2)}) copy-start(bf16[3,3,256,69]{2,3,1,0:T(8,128)(2,1)} %param.5) | copy-start | bytes 953860
  1.6 1.0 %copy-start.3 = (bf16[3,3,69,256]{3,2,1,0:T(8,128)(2,1)S(1)}, bf16[3,3,69,256]{3,2,1,0:T(8,128)(2,1)}, u32[]{:S(2)}) copy-start(bf16[3,3,69,256]{3,2,1,0:T(8,128)(2,1)} %param.6) | copy-start | bytes 953860
  2.6 1.0 %copy-start.4 = (bf16[69,16,128]{2,1,0:T(8,128)(2,1)S(1)}, bf16[69,16,128]{2,1,0:T(8,128)(2,1)}, u32[]{:S(2)}) copy-start(bf16[69,16,128]{2,1,0:T(8,128)(2,1)} %f_hbm.1) | copy-start | bytes 847876
  3.5 1.0 %copy-start.5 = (bf16[69,16,128]{2,1,0:T(8,128)(2,1)S(1)}, bf16[69,16,128]{2,1,0:T(8,128)(2,1)}, u32[]{:S(2)}) copy-start(bf16[69,16,128]{2,1,0:T(8,128)(2,1)} %g_hbm.1) | copy-start | bytes 847876
  40.8 1.0 %copy-start = (bf16[256,16,128]{2,1,0:T(8,128)(2,1)}, bf16[256,16,128]{2,1,0:T(8,128)(2,1)S(1)}, u32[]{:S(2)}) copy-start(bf16[256,16,128]{2,1,0:T(8,128)(2,1)S(1)} %get-tuple-element.12.feat_in) | copy-start | bytes 3145732
  41.8 0.9 %copy-start.1 = (bf16[2,2,16,40,128]{4,3,2,1,0:T(8,128)(2,1)}, bf16[2,2,16,40,128]{4,3,2,1,0:T(8,128)(2,1)S(1)}, u32[]{:S(2)}) copy-start(bf16[2,2,16,40,128]{4,3,2,1,0:T(8,128)(2,1)S(1)} %get-tuple-element.13.grad_in) | copy-start | bytes 1966084
  42.7 0.7 %copy-start.6 = (bf16[69,16,128]{2,1,0:T(8,128)(2,1)}, bf16[69,16,128]{2,1,0:T(8,128)(2,1)S(1)}, u32[]{:S(2)}) copy-start(bf16[69,16,128]{2,1,0:T(8,128)(2,1)S(1)} %get-tuple-element.11.reb_in) | copy-start | bytes 847876
where the time goes:
time: 46.7 us; the launch traced here: 46.4 us
  Pallas kernels  39.3 us (84%)
  local copies, waits for them, and re-layouts  6.4 us (14%)
  between operations  0.66 us (1%)
    pallas_call x1, Pallas kernels, on_device(): pl.pallas_call(functools.partial(layer_kernel, lats, halves, deep), out_s...  36.3 us
    unnamed x14, local copies, waits for them, and re-layouts  6.4 us
    pallas_call x1, Pallas kernels, on_device(): pl.pallas_call(functools.partial(finish_kernel, norm), out_shape=[jax.Sha...  3.02 us

commit v1 on v0

--- a/solution.py
+++ b/solution.py
@@ -553,10 +553,12 @@
             collective_id=0, has_side_effects=True, vmem_limit_bytes=48 << 20
         ),
     )(
+        *(pltpu.with_memory_space_constraint(v, pltpu.HBM) for v in (
         fields,
         recon_grad,
         enc_kernel.transpose(0, 1, 3, 2).reshape(9, count, hid),
         gen_kernel.reshape(9, count, hid),
+        ))
     )
     norm = 1.0 / float(height * lats * width * lons) ** 0.5
     rebuilt, feat, enc_grad, gen_grad = pl.pallas_call(
@@ -574,6 +576,7 @@
             pltpu.VMEM((2, 9, count, hid), F32),
             pltpu.SemaphoreType.DMA((4,)),
         ],
+        compiler_params=pltpu.CompilerParams(vmem_limit_bytes=8 << 20),
     )(rebuilt, feat, summed)
     return (
         rebuilt,

time: 46.7 us -> 38.8 us (0.83)
  local copies, waits for them, and re-layouts: 6.4 us -> 0 us
  Pallas kernels: 39.3 us -> 38 us
    unnamed x14 -> x0, local copies, waits for them, and re-layouts: 6.4 us -> none
    pallas_call x1, Pallas kernels: 3.02 us -> 1.53 us  [on_device(): pl.pallas_call(functools.partial(finish_kernel, norm), out_shape=[jax.Sha...]
where the time goes in v1:
time: 38.8 us; the launch traced here: 38.7 us
  Pallas kernels  38 us (98%)
  between operations  0.64 us (2%)
    pallas_call x1, Pallas kernels, on_device(): pl.pallas_call(functools.partial(layer_kernel, lats, halves, deep), out_s...  36.5 us
    pallas_call x1, Pallas kernels, on_device(): pl.pallas_call(functools.partial(finish_kernel, norm), out_shape=[jax.Sha...  1.53 us

profile of v1, /device:TPU:0, one launch (start us, length us, event | category | flops | bytes accessed | tf_op | source)
XLA Modules:
  0.0 38.7 jit_solution(9468879320451041959)
XLA Ops:
  0.6 36.5 %shard_map.75 = (bf16[69,16,128]{2,1,0:T(8,128)(2,1)S(1)}, bf16[256,16,128]{2,1,0:T(8,128)(2,1)S(1)}, bf16[2,2,16,40,128]{4,3,2,1,0:T(8,128)(2,1)S(1)}) custom-call(bf16[69,16,128]{2,1,0:T(8,128)(2,1)} %f_hbm.1, bf16[69,16,128]{2,1,0:T(8,128)(2,1)} %g_hbm.1, bf16[9,69,256]{2,1,0:T(8,128)(2,1)} %bitcast.8, bf16[9,69,256]{2,1,0:T(8,128)(2,1)} %bitcast.9), custom_call_target="tpu_custom_call" | custom-call | tf_op jit(solution)/shard_map/pallas_call | solution.py:513
  37.1 1.5 %shard_map.76 = (bf16[69,16,128]{2,1,0:T(8,128)(2,1)}, bf16[256,16,128]{2,1,0:T(8,128)(2,1)}, f32[9,69,256]{2,1,0:T(8,128)}, f32[9,69,256]{2,1,0:T(8,128)}) custom-call(bf16[69,16,128]{2,1,0:T(8,128)(2,1)S(1)} %get-tuple-element.11.reb_in, bf16[256,16,128]{2,1,0:T(8,128)(2,1)S(1)} %get-tuple-element.12.feat_in, ...), custom_call_target="tpu_custom_call" | custom-call | tf_op jit(solution)/shard_map/pallas_call | solution.py:564

commit v2 on v1

--- a/solution.py
+++ b/solution.py
@@ -29,8 +29,8 @@
 def layer_kernel(
     lats, halves, deep, f_hbm, g_hbm, we_hbm, wg_hbm, reb_ref, feat_ref, grad_ref,
     fin, win, flat, xg, colp, colh, corner, hrow, dact, feat_rows, wpad, we, wf, wr,
-    ysum, ycol, yhalo, turned, accx, accg, parts, from_pair, lon_out, from_lon, lat_out, from_lat,
-    local_sem, *sems,
+    ysum, ycol, yhalo, turned, accx, accg, parts, from_pair, lon_out, from_lon, lat_out, from_lat, own,
+    local_sem, greeted, *sems,
 ):
     count, height, width = fin.shape[1:]
     hid = hrow.shape[1]
@@ -48,8 +48,23 @@
     def lon_peer(step):
         return (lat, lax.rem(half + step, halves) * 2 + core)
 
-    def lat_peer(step):
-        return (lax.rem(lat + step, lats), lon)
+    def along(step):
+        place = lat + step
+        beyond = jnp.where((place < 0) | (place >= lats), 1, 0)
+        mirrored = 2 * lats - 1 - place if step > 0 else -1 - place
+        return (
+            place + beyond * (mirrored - place),
+            lax.rem(lon + beyond * halves, lons),
+        )
+
+    def greet(level):
+        for step in (1 << level, -(1 << level)):
+            pl.semaphore_signal(
+                greeted.at[level], inc=1, device_id=along(step), device_id_type=MESH
+            )
+
+    def met(level):
+        pl.semaphore_wait(greeted.at[level], 2)
 
     def north_of(place):
         return (lat - below_top, lax.rem(place + (1 - below_top) * halves, lons))
@@ -71,13 +86,6 @@
         (north_of(west_lon), below_top, 1),
     ]
 
-    barrier = pltpu.get_barrier_semaphore()
-    peers = [west, east] + [peer for peer, slot, side in diagonals]
-    peers += [lon_peer(step) for step in range(1, halves)]
-    peers += [lat_peer(step) for step in range(1, lats)]
-    for peer in peers:
-        pl.semaphore_signal(barrier, inc=1, device_id=peer, device_id_type=MESH)
-
     loads = [
         pltpu.make_async_copy(f_hbm, fin.at[0], local_sem.at[0]),
         pltpu.make_async_copy(g_hbm, fin.at[1], local_sem.at[1]),
@@ -86,6 +94,13 @@
     ]
     for load in loads:
         load.start()
+
+    barrier = pltpu.get_barrier_semaphore()
+    peers = [west, east] + [peer for peer, slot, side in diagonals]
+    peers += [lon_peer(step) for step in range(1, halves)]
+    peers += [north, south]
+    for peer in peers:
+        pl.semaphore_signal(barrier, inc=1, device_id=peer, device_id_type=MESH)
 
     def send(src, dst, phase, send_slot, recv_slot, peer):
         copy = pltpu.make_async_remote_copy(
@@ -102,22 +117,28 @@
     def arrive(ref, phase, slot):
         pltpu.make_async_copy(ref, ref, sems[2 * phase + 1].at[slot]).wait()
 
+    def drain(ref, phase, slot):
+        pltpu.make_async_copy(ref, ref, sems[2 * phase].at[slot]).wait()
+
     lane = lax.broadcasted_iota(jnp.int32, (deep, width), 1)
     half_lane = lax.broadcasted_iota(jnp.int32, (half_deep, width), 1)
     rim = (lane == 0) | (lane == width - 1)
 
     for array in range(2):
-        flat[array, count * height :] = jnp.zeros(((deep - count) * height, width), F32)
+        for part in range(height // 8):
+            flat[array, part, count * 8 :] = jnp.zeros(((deep - count) * 8, width), F32)
         wpad[array, :, deep - 16 :] = jnp.zeros((9, 16, hid), BF16)
     accx[...] = jnp.zeros_like(accx)
     accg[...] = jnp.zeros_like(accg)
     for load in loads[:2]:
         load.wait()
     for array in range(2):
-        flat[array, : count * height] = fin[array].astype(F32).reshape(count * height, width)
+        for part in range(height // 8):
+            cells = fin[array, :, part * 8 : (part + 1) * 8].astype(F32)
+            flat[array, part, : count * 8] = cells.reshape(count * 8, width)
 
     def cells_of(array, row):
-        return flat[array, pl.ds(row, deep, stride=height), :]
+        return flat[array, row // 8, pl.ds(row % 8, deep, stride=8), :]
 
     packed = jnp.zeros((half_deep, width), F32)
     for row in range(height):
@@ -157,6 +178,8 @@
         for index, (peer, slot, side) in enumerate(diagonals)
     ]
     row_copies += send_rows(1)
+    levels = greeted.shape[0]
+    greet(0)
 
     for load in loads[2:]:
         load.wait()
@@ -200,10 +223,13 @@
         copy.wait()
     own_rims = join(colh[0], colh[1])
 
+    def centre_of(array, slot):
+        return xg[slot, array * band + deep : array * band + 2 * deep].astype(F32)
+
     def widen_own(array):
         for row in range(height):
             widen(
-                array, row + 1, cells_of(array, row), own_rims,
+                array, row + 1, centre_of(array, row + 1), own_rims,
                 lambda group: -(2 * row + 1 + group),
             )
 
@@ -222,10 +248,10 @@
         for slot in range(2):
             arrive(xg.at[slot * (height + 1), middle], 13, 2 * array + slot)
         for slot in range(2):
-            cells = xg[slot * (height + 1), array * band + deep : array * band + 2 * deep]
+            cells = centre_of(array, slot * (height + 1))
             at = source_rows[slot]
             widen(
-                array, slot * (height + 1), cells.astype(F32), halo_rims[slot],
+                array, slot * (height + 1), cells, halo_rims[slot],
                 lambda group: lax.rem(2 * width - (2 * at + 1 + group), width),
             )
 
@@ -234,6 +260,9 @@
     widen_halo(1)
 
     ends = ((0, below_top, 2 * band, 0), (1, above_end, 0, height - 1))
+    met(0)
+    if levels > 1:
+        greet(1)
     at_poles = []
     for slot, inside, start, row in ends:
         edge = xg[slot * (height + 1), band:]
@@ -276,6 +305,9 @@
 
     for step in range(steps):
         first_step(step)
+    for level in range(1, levels - 1):
+        met(level)
+        greet(level + 1)
     hid_copies = [
         send(hrow.at[1], hrow.at[below_top * (height + 1)], 15, 0, below_top, north),
         send(hrow.at[height], hrow.at[(1 - above_end) * (height + 1)], 15, 1, 1 - above_end, south),
@@ -285,6 +317,12 @@
 
     side_lanes = hid // 2
     per = lon_out.shape[2]
+    owners = lat_out.shape[1]
+    base = (lats - owners) // 2
+    upper = lax.div(2 * lat, lats)
+    owning = (lat >= base) & (lat < base + owners)
+    for stream in range(2):
+        from_lat[stream, lat] = jnp.zeros(from_lat.shape[2:], LINK)
 
     def fill(stream, acc, backward):
         used = 9 * count
@@ -303,12 +341,16 @@
     def piece(index, size):
         return pl.ds(pl.multiple_of(index * size, 8), size)
 
-    order = sorted(range(1, lats), key=lambda step: abs(2 * step - lats))
+    def owner(index):
+        return base + index + upper * (owners - 1 - 2 * index)
+
+    def chunk_of(source, place):
+        return source * owners + place
 
     def start_pair(stream):
         copies = {}
         for step in list(range(1, halves)) + [0]:
-            part = piece(lax.rem(half + step, halves), lats * per)
+            part = piece(lax.rem(half + step, halves), owners * per)
             copies[step] = send(
                 parts.at[stream, other, part], from_pair.at[stream, part], stream * 6, step, step, pair
             )
@@ -319,84 +361,121 @@
         for step in range(1, halves):
             copies[step].wait()
             target = lax.rem(half + step, halves)
-            for turn in order + [0]:
-                there = lax.rem(lat + turn, lats)
-                chunk = target * lats + there
+            for index in reversed(range(owners)):
+                place = owner(index) - base
+                chunk = chunk_of(target, place)
                 part = piece(chunk, per)
                 lon_out[stream, chunk] = (
                     parts[stream, core, part] + from_pair[stream, part]
                 ).astype(LINK)
-                onward[step, turn] = send(
+                slot = (step - 1) * owners + index
+                onward[step, index] = send(
                     lon_out.at[stream, chunk],
-                    from_lon.at[stream, step - 1, there],
-                    stream * 6 + 1, (step - 1) * lats + turn, (step - 1) * lats + turn, lon_peer(step),
+                    from_lon.at[stream, step - 1, place],
+                    stream * 6 + 1, slot, slot, lon_peer(step),
                 )
         copies[0].wait()
         return onward
 
-    def lon_total(stream, copies, turn):
-        there = lax.rem(lat + turn, lats)
-        part = piece(half * lats + there, per)
-        total = parts[stream, core, part] + from_pair[stream, part]
+    def start_lat(stream, copies):
+        for index in reversed(range(owners)):
+            to = owner(index)
+            place = to - base
+            part = piece(chunk_of(half, place), per)
+            total = parts[stream, core, part] + from_pair[stream, part]
+            for step in range(1, halves):
+                copies[step, index].wait()
+                total = total + from_lon[stream, step - 1, place].astype(F32)
+            lat_out[stream, place] = total.astype(LINK)
+
+            @pl.when(to == lat)
+            def _():
+                own[stream] = total
+
+            @pl.when(to != lat)
+            def _():
+                send(
+                    lat_out.at[stream, place], from_lat.at[stream, lat],
+                    stream * 6 + 2, index, lat, (to, lon),
+                )
+
+    def spread(stream, place):
+        mine = grad_ref.at[stream, core, chunk_of(half, place)]
         for step in range(1, halves):
-            copies[step, turn].wait()
-            total = total + from_lon[stream, step - 1, there].astype(F32)
-        return total
-
-    def start_lat(stream, copies):
-        onward = []
-        for turn in order:
-            there = lax.rem(lat + turn, lats)
-            lat_out[stream, there] = lon_total(stream, copies, turn).astype(LINK)
-            onward.append(
-                send(
-                    lat_out.at[stream, there], from_lat.at[stream, turn - 1],
-                    stream * 6 + 2, turn - 1, turn - 1, lat_peer(turn),
-                )
-            )
-        return onward, lon_total(stream, copies, 0)
-
-    def spread(stream, turn, lon_copies, pair_copies):
-        there = lax.rem(lat + lats - turn, lats)
-        mine = grad_ref.at[stream, core, half * lats + there]
-        for step in range(1, halves):
-            slot = (step - 1) * lats + turn
-            lon_copies[step, turn] = send(mine, mine, stream * 6 + 4, slot, slot, lon_peer(step))
-        pair_copies.append(send(mine, mine, stream * 6 + 5, turn, turn, pair))
-
-    def start_lat_gather(stream, started):
-        copies, total = started
-        for turn, copy in zip(order, copies):
-            copy.wait()
-            total = total + from_lat[stream, turn - 1].astype(F32)
-        place = half * lats + lat
-        grad_ref[stream, core, place] = total.astype(grad_ref.dtype)
-        mine = grad_ref.at[stream, core, place]
-        copies = [
-            send(mine, mine, stream * 6 + 3, turn - 1, turn - 1, lat_peer(turn)) for turn in order
-        ]
-        lon_copies, pair_copies = {}, []
-        spread(stream, 0, lon_copies, pair_copies)
-        return copies, lon_copies, pair_copies
-
-    def start_spread(stream, started):
-        copies, lon_copies, pair_copies = started
-        for turn, copy in reversed(list(zip(order, copies))):
-            copy.wait()
-            spread(stream, turn, lon_copies, pair_copies)
-        return lon_copies, pair_copies
-
-    def start_pair_gather(stream, started):
-        lon_copies, pair_copies = started
-        for turn in [0] + order[::-1]:
+            slot = (step - 1) * owners + place
+            send(mine, mine, stream * 6 + 4, slot, slot, lon_peer(step))
+        send(mine, mine, stream * 6 + 5, place, place, pair)
+
+    def far_lat(index):
+        rank = lats - 1 - index if index < lats // 2 else index - lats // 2
+        return rank + upper * (lats - 1 - 2 * rank)
+
+    def start_lat_gather(stream):
+        @pl.when(owning)
+        def _():
+            for source in range(lats):
+
+                @pl.when(source != lat)
+                def _():
+                    arrive(from_lat.at[stream, source], stream * 6 + 2, source)
+
+            total = own[stream]
+            for source in range(lats):
+                total = total + from_lat[stream, source].astype(F32)
+            place = lat - base
+            chunk = chunk_of(half, place)
+            grad_ref[stream, core, chunk] = total.astype(grad_ref.dtype)
+            mine = grad_ref.at[stream, core, chunk]
+            for index in range(lats):
+                to = far_lat(index)
+
+                @pl.when(to != lat)
+                def _():
+                    send(mine, mine, stream * 6 + 3, index, place, (to, lon))
+
+            spread(stream, place)
+
+    def start_spread(stream):
+        for index in range(owners):
+            place = owner(index) - base
+
+            @pl.when(owner(index) != lat)
+            def _():
+                arrive(grad_ref.at[stream, core, chunk_of(half, place)], stream * 6 + 3, place)
+                spread(stream, place)
+
+    def start_pair_gather(stream):
+        for index in range(owners):
+            place = owner(index) - base
             for step in range(1, halves):
-                lon_copies[step, turn].wait()
                 source = lax.rem(half + halves - step, halves)
-                there = lax.rem(lat + lats - turn, lats)
-                mine = grad_ref.at[stream, core, source * lats + there]
-                slot = step * lats + turn
-                pair_copies.append(send(mine, mine, stream * 6 + 5, slot, slot, pair))
-        return pair_copies
+                mine = grad_ref.at[stream, core, chunk_of(source, place)]
+                arrive(mine, stream * 6 + 4, (step - 1) * owners + place)
+                slot = step * owners + place
+                send(mine, mine, stream * 6 + 5, slot, slot, pair)
+
+    def finish(stream):
+        spare = lat_out.at[stream, 0]
+        for place in range(owners):
+            for step in range(halves):
+                source = lax.rem(half + halves - step, halves)
+                slot = step * owners + place
+                arrive(grad_ref.at[stream, other, chunk_of(source, place)], stream * 6 + 5, slot)
+                drain(spare, stream * 6 + 5, slot)
+                if step:
+                    drain(spare, stream * 6 + 4, (step - 1) * owners + place)
+
+            @pl.when(owner(place) != lat)
+            def _():
+                drain(spare, stream * 6 + 2, place)
+
+        @pl.when(owning)
+        def _():
+            for index in range(lats):
+
+                @pl.when(far_lat(index) != lat)
+                def _():
+                    drain(spare, stream * 6 + 3, index)
 
     def pole_term(slot, start):
         return dot(wf[:, start : start + band], at_poles[slot], ((1,), (0,)))
@@ -437,25 +516,33 @@
         return packed
 
     packed = jnp.zeros((deep, width), F32)
-    packed = rebuild_step(0, packed)
     enc_copies = start_lon(1, enc_copies)
-    gen_copies = start_lat(0, gen_copies)
-    for step in range(1, steps):
+    if levels > 1:
+        met(levels - 1)
+    start_lat(0, gen_copies)
+    for step in range(steps):
         packed = rebuild_step(step, packed)
     ycol[...] = packed
     y_copies = [
         send(ycol, yhalo.at[0], 16, 0, 0, east),
         send(ycol, yhalo.at[1], 16, 1, 1, west),
     ]
-    enc_copies = start_lat(1, enc_copies)
+    start_lat(1, enc_copies)
 
     def turn_out(load, target, size):
         for row in range(height):
-            turned[pl.ds(row, size, stride=height), :] = load(row)
-        target[...] = turned[: target.shape[0] * height].reshape(target.shape).astype(BF16)
-
+            turned[row // 8, pl.ds(row % 8, size, stride=8), :] = load(row)
+        kept = target.shape[0]
+        target[...] = jnp.concatenate(
+            [
+                turned[part, : kept * 8].reshape(kept, 8, width)
+                for part in range(height // 8)
+            ],
+            axis=1,
+        ).astype(BF16)
+
+    start_lat_gather(0)
     turn_out(lambda row: feat_rows[row].astype(F32), feat_ref, hid)
-    gen_copies = start_lat_gather(0, gen_copies)
     for copy in y_copies:
         copy.wait()
     y_rims = jnp.where(lax.rem(lane, 2) == 0, shifted(yhalo[1], -1), shifted(yhalo[0], 1))
@@ -464,14 +551,14 @@
         edges = shifted(y_rims, -(2 * row + 1))
         return ysum[row] + jnp.where((lane == 0) | (lane == width - 1), edges, 0.0)
 
+    start_lat_gather(1)
     turn_out(rebuilt_row, reb_ref, deep)
-    enc_copies = start_lat_gather(1, enc_copies)
-    gen_copies = start_spread(0, gen_copies)
-    gen_copies = start_pair_gather(0, gen_copies)
-    enc_copies = start_spread(1, enc_copies)
-    enc_copies = start_pair_gather(1, enc_copies)
-    for copy in gen_copies + enc_copies:
-        copy.wait()
+    start_spread(0)
+    start_pair_gather(0)
+    start_spread(1)
+    start_pair_gather(1)
+    finish(0)
+    finish(1)
 
 
 def finish_kernel(norm, reb_in, feat_in, grad_in, reb_out, feat_out, enc_out, gen_out, flat, ready, sem):
@@ -504,10 +591,12 @@
     halves = lons // 2
     band = 3 * deep
     side_lanes = hid // 2
-    chunks = halves * lats
+    owners = max(lats // 2, 1)
+    chunks = halves * owners
     per = -(-9 * count // (chunks * 8)) * 8
-    hops = (halves - 1) * lats
-    counts = [halves, hops, lats - 1, lats - 1, hops, chunks] * 2 + [2, 4, 4, 2, 2]
+    hops = (halves - 1) * owners
+    levels = (lats - 1).bit_length()
+    counts = [halves, hops, lats, lats, hops, chunks] * 2 + [2, 4, 4, 2, 2]
     vmem = pl.BlockSpec(memory_space=pltpu.VMEM)
     anywhere = pl.BlockSpec(memory_space=pltpu.HBM)
     rebuilt, feat, summed = pl.pallas_call(
@@ -522,7 +611,7 @@
         scratch_shapes=[
             pltpu.VMEM((2, count, height, width), BF16),
             pltpu.VMEM((2, 9, count, hid), BF16),
-            pltpu.VMEM((2, deep * height, width), F32),
+            pltpu.VMEM((2, height // 8, deep * 8, width), F32),
             pltpu.VMEM((height + 2, 2 * band, width), BF16),
             pltpu.VMEM((deep // 2, width), BF16),
             pltpu.VMEM((2, deep // 2, width), BF16),
@@ -537,16 +626,18 @@
             pltpu.VMEM((height, deep, width), F32),
             pltpu.VMEM((deep, width), F32),
             pltpu.VMEM((2, deep, width), F32),
-            pltpu.VMEM((hid * height, width), F32),
+            pltpu.VMEM((height // 8, hid * 8, width), F32),
             pltpu.VMEM((9 * deep, hid), F32),
             pltpu.VMEM((9 * deep, hid), F32),
             pltpu.VMEM((2, 2, chunks * per, side_lanes), F32),
             pltpu.VMEM((2, chunks * per, side_lanes), F32),
             pltpu.VMEM((2, chunks, per, side_lanes), LINK),
-            pltpu.VMEM((2, halves - 1, lats, per, side_lanes), LINK),
+            pltpu.VMEM((2, halves - 1, owners, per, side_lanes), LINK),
+            pltpu.VMEM((2, owners, per, side_lanes), LINK),
             pltpu.VMEM((2, lats, per, side_lanes), LINK),
-            pltpu.VMEM((2, lats - 1, per, side_lanes), LINK),
+            pltpu.VMEM((2, per, side_lanes), F32),
             pltpu.SemaphoreType.DMA((4,)),
+            pltpu.SemaphoreType.REGULAR((levels,)),
         ]
         + [pltpu.SemaphoreType.DMA((size,)) for size in counts for _ in range(2)],
         compiler_params=pltpu.CompilerParams(

time: 38.8 us -> 36.5 us (0.941)
  Pallas kernels: 38 us -> 35.7 us
    pallas_call x1, Pallas kernels: 36.5 us -> 34.2 us  [on_device(): pl.pallas_call(functools.partial(layer_kernel, lats, halves, deep), out_s...]
where the time goes in v2:
time: 36.5 us; the launch traced here: 36.3 us
  Pallas kernels  35.7 us (98%)
  between operations  0.64 us (2%)
    pallas_call x1, Pallas kernels, on_device(): pl.pallas_call(functools.partial(layer_kernel, lats, halves, deep), out_s...  34.2 us
    pallas_call x1, Pallas kernels, on_device(): pl.pallas_call(functools.partial(finish_kernel, norm), out_shape=[jax.Sha...  1.53 us

profile of v2, /device:TPU:0, one launch (start us, length us, event | category | flops | bytes accessed | tf_op | source)
XLA Modules:
  0.0 36.3 jit_solution(10064007821715549509)
XLA Ops:
  0.6 34.2 %shard_map.75 = (bf16[69,16,128]{2,1,0:T(8,128)(2,1)S(1)}, bf16[256,16,128]{2,1,0:T(8,128)(2,1)S(1)}, bf16[2,2,8,80,128]{4,3,2,1,0:T(8,128)(2,1)S(1)}) custom-call(bf16[69,16,128]{2,1,0:T(8,128)(2,1)} %f_hbm.1, bf16[69,16,128]{2,1,0:T(8,128)(2,1)} %g_hbm.1, bf16[9,69,256]{2,1,0:T(8,128)(2,1)} %bitcast.8, bf16[9,69,256]{2,1,0:T(8,128)(2,1)} %bitcast.9), custom_call_target="tpu_custom_call" | custom-call | tf_op jit(solution)/shard_map/pallas_call | solution.py:602
  34.8 1.5 %shard_map.76 = (bf16[69,16,128]{2,1,0:T(8,128)(2,1)}, bf16[256,16,128]{2,1,0:T(8,128)(2,1)}, f32[9,69,256]{2,1,0:T(8,128)}, f32[9,69,256]{2,1,0:T(8,128)}) custom-call(bf16[69,16,128]{2,1,0:T(8,128)(2,1)S(1)} %get-tuple-element.11.reb_in, bf16[256,16,128]{2,1,0:T(8,128)(2,1)S(1)} %get-tuple-element.12.feat_in, ...), custom_call_target="tpu_custom_call" | custom-call | tf_op jit(solution)/shard_map/pallas_call | solution.py:655

commit v3 on v2

--- a/solution.py
+++ b/solution.py
@@ -45,8 +45,17 @@
     below_top = lax.div(lat + lats - 1, lats)
     above_end = lax.div(2 * lats - 2 - lat, lats)
 
-    def lon_peer(step):
-        return (lat, lax.rem(half + step, halves) * 2 + core)
+    inner = lats // from_lat.shape[1]
+    plane = halves * inner
+    level_at = lax.div(lat, inner)
+    row_at = lax.rem(lat, inner)
+
+    def plane_peer(index):
+        turn, swap = divmod(index, inner)
+        return (
+            level_at * inner + lax.rem(row_at + swap, inner),
+            lax.rem(half + turn, halves) * 2 + core,
+        )
 
     def along(step):
         place = lat + step
@@ -97,7 +106,7 @@
 
     barrier = pltpu.get_barrier_semaphore()
     peers = [west, east] + [peer for peer, slot, side in diagonals]
-    peers += [lon_peer(step) for step in range(1, halves)]
+    peers += [plane_peer(index) for index in range(1, plane)]
     peers += [north, south]
     for peer in peers:
         pl.semaphore_signal(barrier, inc=1, device_id=peer, device_id_type=MESH)
@@ -233,17 +242,9 @@
                 lambda group: -(2 * row + 1 + group),
             )
 
-    widen_own(0)
-    for copy in corner_copies:
-        copy.wait_send()
-    for slot in range(4):
-        arrive(corner.at[slot // 2, slot % 2], 14, slot)
-    for copy in row_copies:
-        copy.wait_send()
-    halo_rims = [join(corner[slot, 0], corner[slot, 1]) for slot in range(2)]
     source_rows = (below_top * (height - 1), (1 - above_end) * (height - 1))
 
-    def widen_halo(array):
+    def widen_halo(array, halo_rims):
         middle = pl.ds(array * band + deep, deep)
         for slot in range(2):
             arrive(xg.at[slot * (height + 1), middle], 13, 2 * array + slot)
@@ -255,20 +256,6 @@
                 lambda group: lax.rem(2 * width - (2 * at + 1 + group), width),
             )
 
-    widen_halo(0)
-    widen_own(1)
-    widen_halo(1)
-
-    ends = ((0, below_top, 2 * band, 0), (1, above_end, 0, height - 1))
-    met(0)
-    if levels > 1:
-        greet(1)
-    at_poles = []
-    for slot, inside, start, row in ends:
-        edge = xg[slot * (height + 1), band:]
-        at_poles.append(jnp.where(inside == 0, edge, jnp.zeros_like(edge)))
-        xg[slot * (height + 1), band:] = jnp.where(inside == 0, jnp.zeros_like(edge), edge)
-
     rows = 4
     steps = height // rows
 
@@ -281,7 +268,7 @@
             axis=1,
         )
 
-    def first_step(step):
+    def conv_step(step):
         row = step * rows
         pre_act = dot(we[...], window(xg, row, 0, band), ((1,), (0,)))
         logistic = 1.0 / (1.0 + jnp.exp(-pre_act))
@@ -290,6 +277,10 @@
         hidden = gated.astype(BF16)
         for place in range(rows):
             hrow[row + 1 + place] = hidden[:, place * width : (place + 1) * width]
+
+    def gen_step(step):
+        row = step * rows
+        hidden = jnp.concatenate([hrow[row + 1 + place] for place in range(rows)], axis=1)
         accg[...] += dot(window(xg, row, band, band), hidden, ((1,), (1,)))
 
     def second_step(step, extra):
@@ -303,26 +294,51 @@
         pre_grad = (feat.astype(F32) * dact[step]).astype(BF16)
         accx[...] += dot(window(xg, row, 0, band), pre_grad, ((1,), (1,)))
 
-    for step in range(steps):
-        first_step(step)
+    widen_own(0)
+    met(0)
+    if levels > 1:
+        greet(1)
+    for step in range(1, steps - 1):
+        conv_step(step)
+    widen_own(1)
+    for copy in corner_copies:
+        copy.wait_send()
+    for slot in range(4):
+        arrive(corner.at[slot // 2, slot % 2], 14, slot)
+    for copy in row_copies:
+        copy.wait_send()
+    halo_rims = [join(corner[slot, 0], corner[slot, 1]) for slot in range(2)]
+    widen_halo(0, halo_rims)
     for level in range(1, levels - 1):
         met(level)
         greet(level + 1)
+    conv_step(0)
+    conv_step(steps - 1)
     hid_copies = [
         send(hrow.at[1], hrow.at[below_top * (height + 1)], 15, 0, below_top, north),
         send(hrow.at[height], hrow.at[(1 - above_end) * (height + 1)], 15, 1, 1 - above_end, south),
     ]
+    widen_halo(1, halo_rims)
+    ends = ((0, below_top, 2 * band, 0), (1, above_end, 0, height - 1))
+    at_poles = []
+    for slot, inside, start, row in ends:
+        edge = xg[slot * (height + 1), band:]
+        at_poles.append(jnp.where(inside == 0, edge, jnp.zeros_like(edge)))
+        xg[slot * (height + 1), band:] = jnp.where(inside == 0, jnp.zeros_like(edge), edge)
+    for step in range(steps):
+        gen_step(step)
     for slot, inside, start, row in ends:
         accg[start : start + band] += dot(at_poles[slot], hrow[row + 1], ((1,), (1,)))
 
     side_lanes = hid // 2
     per = lon_out.shape[2]
     owners = lat_out.shape[1]
-    base = (lats - owners) // 2
-    upper = lax.div(2 * lat, lats)
-    owning = (lat >= base) & (lat < base + owners)
+    tall = from_lat.shape[1]
+    base = (tall - owners) // 2
+    upper = lax.div(2 * level_at, tall)
+    owning = (level_at >= base) & (level_at < base + owners)
     for stream in range(2):
-        from_lat[stream, lat] = jnp.zeros(from_lat.shape[2:], LINK)
+        from_lat[stream, level_at] = jnp.zeros(from_lat.shape[2:], LINK)
 
     def fill(stream, acc, backward):
         used = 9 * count
@@ -344,136 +360,138 @@
     def owner(index):
         return base + index + upper * (owners - 1 - 2 * index)
 
-    def chunk_of(source, place):
-        return source * owners + place
+    def block_of(index, forward):
+        turn, swap = divmod(index, inner)
+        source = lax.rem(half + (turn if forward else halves - turn), halves)
+        return source * inner + lax.rem(row_at + swap, inner)
 
     def start_pair(stream):
         copies = {}
-        for step in list(range(1, halves)) + [0]:
-            part = piece(lax.rem(half + step, halves), owners * per)
-            copies[step] = send(
-                parts.at[stream, other, part], from_pair.at[stream, part], stream * 6, step, step, pair
+        for index in list(range(plane - 1, 0, -1)) + [0]:
+            part = piece(block_of(index, True), owners * per)
+            copies[index] = send(
+                parts.at[stream, other, part], from_pair.at[stream, part],
+                stream * 6, index, index, pair,
             )
         return copies
 
     def start_lon(stream, copies):
         onward = {}
-        for step in range(1, halves):
-            copies[step].wait()
-            target = lax.rem(half + step, halves)
-            for index in reversed(range(owners)):
-                place = owner(index) - base
-                chunk = chunk_of(target, place)
+        for index in range(plane - 1, 0, -1):
+            copies[index].wait()
+            for rank in reversed(range(owners)):
+                place = owner(rank) - base
+                chunk = block_of(index, True) * owners + place
                 part = piece(chunk, per)
                 lon_out[stream, chunk] = (
                     parts[stream, core, part] + from_pair[stream, part]
                 ).astype(LINK)
-                slot = (step - 1) * owners + index
-                onward[step, index] = send(
+                slot = (index - 1) * owners + rank
+                onward[index, rank] = send(
                     lon_out.at[stream, chunk],
-                    from_lon.at[stream, step - 1, place],
-                    stream * 6 + 1, slot, slot, lon_peer(step),
+                    from_lon.at[stream, index - 1, place],
+                    stream * 6 + 1, slot, slot, plane_peer(index),
                 )
         copies[0].wait()
         return onward
 
     def start_lat(stream, copies):
-        for index in reversed(range(owners)):
-            to = owner(index)
+        for rank in reversed(range(owners)):
+            to = owner(rank)
             place = to - base
-            part = piece(chunk_of(half, place), per)
+            part = piece(block_of(0, True) * owners + place, per)
             total = parts[stream, core, part] + from_pair[stream, part]
-            for step in range(1, halves):
-                copies[step, index].wait()
-                total = total + from_lon[stream, step - 1, place].astype(F32)
+            for index in range(plane - 1, 0, -1):
+                copies[index, rank].wait()
+                total = total + from_lon[stream, index - 1, place].astype(F32)
             lat_out[stream, place] = total.astype(LINK)
 
-            @pl.when(to == lat)
+            @pl.when(to == level_at)
             def _():
                 own[stream] = total
 
-            @pl.when(to != lat)
+            @pl.when(to != level_at)
             def _():
                 send(
-                    lat_out.at[stream, place], from_lat.at[stream, lat],
-                    stream * 6 + 2, index, lat, (to, lon),
+                    lat_out.at[stream, place], from_lat.at[stream, level_at],
+                    stream * 6 + 2, rank, level_at, (to * inner + row_at, lon),
                 )
 
     def spread(stream, place):
-        mine = grad_ref.at[stream, core, chunk_of(half, place)]
-        for step in range(1, halves):
-            slot = (step - 1) * owners + place
-            send(mine, mine, stream * 6 + 4, slot, slot, lon_peer(step))
+        mine = grad_ref.at[stream, core, block_of(0, True) * owners + place]
+        for index in range(plane - 1, 0, -1):
+            slot = (index - 1) * owners + place
+            send(mine, mine, stream * 6 + 4, slot, slot, plane_peer(index))
         send(mine, mine, stream * 6 + 5, place, place, pair)
 
-    def far_lat(index):
-        rank = lats - 1 - index if index < lats // 2 else index - lats // 2
-        return rank + upper * (lats - 1 - 2 * rank)
+    def far_level(index):
+        rank = tall - 1 - index if index < tall // 2 else index - tall // 2
+        return rank + upper * (tall - 1 - 2 * rank)
 
     def start_lat_gather(stream):
         @pl.when(owning)
         def _():
-            for source in range(lats):
-
-                @pl.when(source != lat)
+            for source in range(tall):
+
+                @pl.when(source != level_at)
                 def _():
                     arrive(from_lat.at[stream, source], stream * 6 + 2, source)
 
             total = own[stream]
-            for source in range(lats):
+            for source in range(tall):
                 total = total + from_lat[stream, source].astype(F32)
-            place = lat - base
-            chunk = chunk_of(half, place)
+            place = level_at - base
+            chunk = block_of(0, True) * owners + place
             grad_ref[stream, core, chunk] = total.astype(grad_ref.dtype)
             mine = grad_ref.at[stream, core, chunk]
-            for index in range(lats):
-                to = far_lat(index)
-
-                @pl.when(to != lat)
+            for index in range(tall):
+                to = far_level(index)
+
+                @pl.when(to != level_at)
                 def _():
-                    send(mine, mine, stream * 6 + 3, index, place, (to, lon))
+                    send(mine, mine, stream * 6 + 3, index, place, (to * inner + row_at, lon))
 
             spread(stream, place)
 
     def start_spread(stream):
-        for index in range(owners):
-            place = owner(index) - base
-
-            @pl.when(owner(index) != lat)
+        for rank in range(owners):
+            place = owner(rank) - base
+
+            @pl.when(owner(rank) != level_at)
             def _():
-                arrive(grad_ref.at[stream, core, chunk_of(half, place)], stream * 6 + 3, place)
+                chunk = block_of(0, True) * owners + place
+                arrive(grad_ref.at[stream, core, chunk], stream * 6 + 3, place)
                 spread(stream, place)
 
     def start_pair_gather(stream):
-        for index in range(owners):
-            place = owner(index) - base
-            for step in range(1, halves):
-                source = lax.rem(half + halves - step, halves)
-                mine = grad_ref.at[stream, core, chunk_of(source, place)]
-                arrive(mine, stream * 6 + 4, (step - 1) * owners + place)
-                slot = step * owners + place
+        for rank in range(owners):
+            place = owner(rank) - base
+            for index in range(1, plane):
+                mine = grad_ref.at[stream, core, block_of(index, False) * owners + place]
+                arrive(mine, stream * 6 + 4, (index - 1) * owners + place)
+                slot = index * owners + place
                 send(mine, mine, stream * 6 + 5, slot, slot, pair)
 
     def finish(stream):
         spare = lat_out.at[stream, 0]
         for place in range(owners):
-            for step in range(halves):
-                source = lax.rem(half + halves - step, halves)
-                slot = step * owners + place
-                arrive(grad_ref.at[stream, other, chunk_of(source, place)], stream * 6 + 5, slot)
+            for index in range(plane):
+                chunk = block_of(index, False) * owners + place
+                slot = index * owners + place
+                arrive(grad_ref.at[stream, other, chunk], stream * 6 + 5, slot)
                 drain(spare, stream * 6 + 5, slot)
-                if step:
-                    drain(spare, stream * 6 + 4, (step - 1) * owners + place)
-
-            @pl.when(owner(place) != lat)
+                if index:
+                    drain(spare, stream * 6 + 4, (index - 1) * owners + place)
+
+            @pl.when(owner(place) != level_at)
             def _():
                 drain(spare, stream * 6 + 2, place)
 
         @pl.when(owning)
         def _():
-            for index in range(lats):
-
-                @pl.when(far_lat(index) != lat)
+            for index in range(tall):
+
+                @pl.when(far_level(index) != level_at)
                 def _():
                     drain(spare, stream * 6 + 3, index)
 
@@ -554,8 +572,8 @@
     start_lat_gather(1)
     turn_out(rebuilt_row, reb_ref, deep)
     start_spread(0)
+    start_spread(1)
     start_pair_gather(0)
-    start_spread(1)
     start_pair_gather(1)
     finish(0)
     finish(1)
@@ -591,12 +609,16 @@
     halves = lons // 2
     band = 3 * deep
     side_lanes = hid // 2
-    owners = max(lats // 2, 1)
-    chunks = halves * owners
+    inner = 2
+    tall = lats // inner
+    owners = tall // 2
+    plane = halves * inner
+    chunks = plane * owners
     per = -(-9 * count // (chunks * 8)) * 8
-    hops = (halves - 1) * owners
-    levels = (lats - 1).bit_length()
-    counts = [halves, hops, lats, lats, hops, chunks] * 2 + [2, 4, 4, 2, 2]
+    hops = (plane - 1) * owners
+    reach = inner * (tall - 1 - (tall - owners) // 2)
+    levels = (reach - 1).bit_length()
+    counts = [plane, hops, tall, tall, hops, chunks] * 2 + [2, 4, 4, 2, 2]
     vmem = pl.BlockSpec(memory_space=pltpu.VMEM)
     anywhere = pl.BlockSpec(memory_space=pltpu.HBM)
     rebuilt, feat, summed = pl.pallas_call(
@@ -632,9 +654,9 @@
             pltpu.VMEM((2, 2, chunks * per, side_lanes), F32),
             pltpu.VMEM((2, chunks * per, side_lanes), F32),
             pltpu.VMEM((2, chunks, per, side_lanes), LINK),
-            pltpu.VMEM((2, halves - 1, owners, per, side_lanes), LINK),
+            pltpu.VMEM((2, plane - 1, owners, per, side_lanes), LINK),
             pltpu.VMEM((2, owners, per, side_lanes), LINK),
-            pltpu.VMEM((2, lats, per, side_lanes), LINK),
+            pltpu.VMEM((2, tall, per, side_lanes), LINK),
             pltpu.VMEM((2, per, side_lanes), F32),
             pltpu.SemaphoreType.DMA((4,)),
             pltpu.SemaphoreType.REGULAR((levels,)),

time: 36.5 us -> 34.2 us (0.937)
  Pallas kernels: 35.7 us -> 33.5 us
    pallas_call x1, Pallas kernels: 34.2 us -> 31.9 us  [on_device(): pl.pallas_call(functools.partial(layer_kernel, lats, halves, deep), out_s...]
where the time goes in v3:
time: 34.2 us; the launch traced here: 34.1 us
  Pallas kernels  33.5 us (98%)
  between operations  0.64 us (2%)
    pallas_call x1, Pallas kernels, on_device(): pl.pallas_call(functools.partial(layer_kernel, lats, halves, deep), out_s...  31.9 us
    pallas_call x1, Pallas kernels, on_device(): pl.pallas_call(functools.partial(finish_kernel, norm), out_shape=[jax.Sha...  1.53 us

profile of v3, /device:TPU:0, one launch (start us, length us, event | category | flops | bytes accessed | tf_op | source)
XLA Modules:
  0.0 34.1 jit_solution(14328452146601320722)
XLA Ops:
  0.6 31.9 %shard_map.75 = (bf16[69,16,128]{2,1,0:T(8,128)(2,1)S(1)}, bf16[256,16,128]{2,1,0:T(8,128)(2,1)S(1)}, bf16[2,2,8,80,128]{4,3,2,1,0:T(8,128)(2,1)S(1)}) custom-call(bf16[69,16,128]{2,1,0:T(8,128)(2,1)} %f_hbm.1, bf16[69,16,128]{2,1,0:T(8,128)(2,1)} %g_hbm.1, bf16[9,69,256]{2,1,0:T(8,128)(2,1)} %bitcast.8, bf16[9,69,256]{2,1,0:T(8,128)(2,1)} %bitcast.9), custom_call_target="tpu_custom_call" | custom-call | tf_op jit(solution)/shard_map/pallas_call | solution.py:624
  32.6 1.5 %shard_map.76 = (bf16[69,16,128]{2,1,0:T(8,128)(2,1)}, bf16[256,16,128]{2,1,0:T(8,128)(2,1)}, f32[9,69,256]{2,1,0:T(8,128)}, f32[9,69,256]{2,1,0:T(8,128)}) custom-call(bf16[69,16,128]{2,1,0:T(8,128)(2,1)S(1)} %get-tuple-element.11.reb_in, bf16[256,16,128]{2,1,0:T(8,128)(2,1)S(1)} %get-tuple-element.12.feat_in, ...), custom_call_target="tpu_custom_call" | custom-call | tf_op jit(solution)/shard_map/pallas_call | solution.py:677

commit v4 on v3

--- a/solution.py
+++ b/solution.py
@@ -499,7 +499,6 @@
         return dot(wf[:, start : start + band], at_poles[slot], ((1,), (0,)))
 
     fill(0, accg, True)
-    gen_copies = start_pair(0)
     open_gap = jnp.zeros((hid, (rows - 1) * width), F32)
     for step in range(steps):
         extra = None
@@ -508,7 +507,9 @@
         elif step == steps - 1:
             extra = jnp.concatenate([open_gap, pole_term(1, 0)], axis=1)
         second_step(step, extra)
-        if step == 1:
+        if step == 0:
+            gen_copies = start_pair(0)
+        if step == 2:
             gen_copies = start_lon(0, gen_copies)
     fill(1, accx, False)
     enc_copies = start_pair(1)

time: 34.2 us -> 33.7 us (0.985)
  Pallas kernels: 33.5 us -> 32.9 us
    pallas_call x1, Pallas kernels: 31.9 us -> 31.3 us  [on_device(): pl.pallas_call(functools.partial(layer_kernel, lats, halves, deep), out_s...]
where the time goes in v4:
time: 33.7 us; the launch traced here: 33.5 us
  Pallas kernels  32.9 us (98%)
  between operations  0.64 us (2%)
    pallas_call x1, Pallas kernels, on_device(): pl.pallas_call(functools.partial(layer_kernel, lats, halves, deep), out_s...  31.3 us
    pallas_call x1, Pallas kernels, on_device(): pl.pallas_call(functools.partial(finish_kernel, norm), out_shape=[jax.Sha...  1.53 us

profile of v4, /device:TPU:0, one launch (start us, length us, event | category | flops | bytes accessed | tf_op | source)
XLA Modules:
  0.0 33.5 jit_solution(5619983381334953293)
XLA Ops:
  0.6 31.3 %shard_map.75 = (bf16[69,16,128]{2,1,0:T(8,128)(2,1)S(1)}, bf16[256,16,128]{2,1,0:T(8,128)(2,1)S(1)}, bf16[2,2,8,80,128]{4,3,2,1,0:T(8,128)(2,1)S(1)}) custom-call(bf16[69,16,128]{2,1,0:T(8,128)(2,1)} %f_hbm.1, bf16[69,16,128]{2,1,0:T(8,128)(2,1)} %g_hbm.1, bf16[9,69,256]{2,1,0:T(8,128)(2,1)} %bitcast.8, bf16[9,69,256]{2,1,0:T(8,128)(2,1)} %bitcast.9), custom_call_target="tpu_custom_call" | custom-call | tf_op jit(solution)/shard_map/pallas_call | solution.py:625
  32.0 1.5 %shard_map.76 = (bf16[69,16,128]{2,1,0:T(8,128)(2,1)}, bf16[256,16,128]{2,1,0:T(8,128)(2,1)}, f32[9,69,256]{2,1,0:T(8,128)}, f32[9,69,256]{2,1,0:T(8,128)}) custom-call(bf16[69,16,128]{2,1,0:T(8,128)(2,1)S(1)} %get-tuple-element.11.reb_in, bf16[256,16,128]{2,1,0:T(8,128)(2,1)S(1)} %get-tuple-element.12.feat_in, ...), custom_call_target="tpu_custom_call" | custom-call | tf_op jit(solution)/shard_map/pallas_call | solution.py:678

commit v5 on v4

--- a/solution.py
+++ b/solution.py
@@ -29,7 +29,7 @@
 def layer_kernel(
     lats, halves, deep, f_hbm, g_hbm, we_hbm, wg_hbm, reb_ref, feat_ref, grad_ref,
     fin, win, flat, xg, colp, colh, corner, hrow, dact, feat_rows, wpad, we, wf, wr,
-    ysum, ycol, yhalo, turned, accx, accg, parts, from_pair, lon_out, from_lon, lat_out, from_lat, own,
+    ysum, ycol, yhalo, turned, pregrad, parts, from_pair, lon_out, from_lon, lat_out, from_lat, own,
     local_sem, greeted, *sems,
 ):
     count, height, width = fin.shape[1:]
@@ -137,8 +137,6 @@
         for part in range(height // 8):
             flat[array, part, count * 8 :] = jnp.zeros(((deep - count) * 8, width), F32)
         wpad[array, :, deep - 16 :] = jnp.zeros((9, 16, hid), BF16)
-    accx[...] = jnp.zeros_like(accx)
-    accg[...] = jnp.zeros_like(accg)
     for load in loads[:2]:
         load.wait()
     for array in range(2):
@@ -278,11 +276,6 @@
         for place in range(rows):
             hrow[row + 1 + place] = hidden[:, place * width : (place + 1) * width]
 
-    def gen_step(step):
-        row = step * rows
-        hidden = jnp.concatenate([hrow[row + 1 + place] for place in range(rows)], axis=1)
-        accg[...] += dot(window(xg, row, band, band), hidden, ((1,), (1,)))
-
     def second_step(step, extra):
         row = step * rows
         feat = dot(wf[...], window(xg, row, band, band), ((1,), (0,)))
@@ -292,7 +285,7 @@
         for place in range(rows):
             feat_rows[row + place] = feat[:, place * width : (place + 1) * width]
         pre_grad = (feat.astype(F32) * dact[step]).astype(BF16)
-        accx[...] += dot(window(xg, row, 0, band), pre_grad, ((1,), (1,)))
+        pregrad[:, step * rows * width : (step + 1) * rows * width] = pre_grad
 
     widen_own(0)
     met(0)
@@ -325,11 +318,6 @@
         edge = xg[slot * (height + 1), band:]
         at_poles.append(jnp.where(inside == 0, edge, jnp.zeros_like(edge)))
         xg[slot * (height + 1), band:] = jnp.where(inside == 0, jnp.zeros_like(edge), edge)
-    for step in range(steps):
-        gen_step(step)
-    for slot, inside, start, row in ends:
-        accg[start : start + band] += dot(at_poles[slot], hrow[row + 1], ((1,), (1,)))
-
     side_lanes = hid // 2
     per = lon_out.shape[2]
     owners = lat_out.shape[1]
@@ -340,19 +328,19 @@
     for stream in range(2):
         from_lat[stream, level_at] = jnp.zeros(from_lat.shape[2:], LINK)
 
-    def fill(stream, acc, backward):
-        used = 9 * count
-        for tap in range(9):
-            row_tap, col_tap = divmod(tap, 3)
-            source = ((2 - row_tap) * 3 + col_tap if backward else tap) * deep
+    def fill(stream, row_tap, value):
+        for col_tap in range(3):
+            tap = row_tap * 3 + col_tap
             for side in range(2):
-                parts[stream, side, tap * count : (tap + 1) * count] = acc[
-                    source : source + count, side * side_lanes : (side + 1) * side_lanes
+                parts[stream, side, tap * count : (tap + 1) * count] = value[
+                    col_tap * deep : col_tap * deep + count,
+                    side * side_lanes : (side + 1) * side_lanes,
                 ]
-        spare = parts.shape[2] - used
-        if spare:
-            for side in range(2):
-                parts[stream, side, used:] = jnp.zeros((spare, side_lanes), F32)
+
+    def rows_at(place, start):
+        return jnp.concatenate(
+            [xg[row + place, start : start + band] for row in range(height)], axis=1
+        )
 
     def piece(index, size):
         return pl.ds(pl.multiple_of(index * size, 8), size)
@@ -498,7 +486,18 @@
     def pole_term(slot, start):
         return dot(wf[:, start : start + band], at_poles[slot], ((1,), (0,)))
 
-    fill(0, accg, True)
+    spare_rows = parts.shape[2] - 9 * count
+    if spare_rows:
+        for stream in range(2):
+            for side in range(2):
+                parts[stream, side, 9 * count :] = jnp.zeros((spare_rows, side_lanes), F32)
+    hidden = jnp.concatenate([hrow[row + 1] for row in range(height)], axis=1)
+    for place in range(3):
+        value = dot(rows_at(place, band), hidden, ((1,), (1,)))
+        for slot, inside, start, row in ends:
+            if start == place * band:
+                value = value + dot(at_poles[slot], hrow[row + 1], ((1,), (1,)))
+        fill(0, 2 - place, value)
     open_gap = jnp.zeros((hid, (rows - 1) * width), F32)
     for step in range(steps):
         extra = None
@@ -509,15 +508,11 @@
         second_step(step, extra)
         if step == 0:
             gen_copies = start_pair(0)
-        if step == 2:
+        if step == 3:
             gen_copies = start_lon(0, gen_copies)
-    fill(1, accx, False)
+    for place in range(3):
+        fill(1, place, dot(rows_at(place, 0), pregrad[...], ((1,), (1,))))
     enc_copies = start_pair(1)
-
-    for copy in hid_copies:
-        copy.wait_send()
-    for slot in range(2):
-        arrive(hrow.at[slot * (height + 1)], 15, slot)
 
     def rebuild_step(step, packed):
         value = dot(wr[...], window(hrow, step * rows, 0, hid), ((1,), (0,)))
@@ -539,6 +534,10 @@
     if levels > 1:
         met(levels - 1)
     start_lat(0, gen_copies)
+    for copy in hid_copies:
+        copy.wait_send()
+    for slot in range(2):
+        arrive(hrow.at[slot * (height + 1)], 15, slot)
     for step in range(steps):
         packed = rebuild_step(step, packed)
     ycol[...] = packed
@@ -650,8 +649,7 @@
             pltpu.VMEM((deep, width), F32),
             pltpu.VMEM((2, deep, width), F32),
             pltpu.VMEM((height // 8, hid * 8, width), F32),
-            pltpu.VMEM((9 * deep, hid), F32),
-            pltpu.VMEM((9 * deep, hid), F32),
+            pltpu.VMEM((hid, height * width), BF16),
             pltpu.VMEM((2, 2, chunks * per, side_lanes), F32),
             pltpu.VMEM((2, chunks * per, side_lanes), F32),
             pltpu.VMEM((2, chunks, per, side_lanes), LINK),

time: 33.7 us -> 33.3 us (0.988)
  Pallas kernels: 32.9 us -> 32.5 us
    pallas_call x1, Pallas kernels: 31.3 us -> 31 us  [on_device(): pl.pallas_call(functools.partial(layer_kernel, lats, halves, deep), out_s...]
where the time goes in v5:
time: 33.3 us; the launch traced here: 33.1 us
  Pallas kernels  32.5 us (98%)
  between operations  0.64 us (2%)
    pallas_call x1, Pallas kernels, on_device(): pl.pallas_call(functools.partial(layer_kernel, lats, halves, deep), out_s...  31 us
    pallas_call x1, Pallas kernels, on_device(): pl.pallas_call(functools.partial(finish_kernel, norm), out_shape=[jax.Sha...  1.53 us

profile of v5, /device:TPU:0, one launch (start us, length us, event | category | flops | bytes accessed | tf_op | source)
XLA Modules:
  0.0 33.1 jit_solution(6922551487558563899)
XLA Ops:
  0.6 31.0 %shard_map.75 = (bf16[69,16,128]{2,1,0:T(8,128)(2,1)S(1)}, bf16[256,16,128]{2,1,0:T(8,128)(2,1)S(1)}, bf16[2,2,8,80,128]{4,3,2,1,0:T(8,128)(2,1)S(1)}) custom-call(bf16[69,16,128]{2,1,0:T(8,128)(2,1)} %f_hbm.1, bf16[69,16,128]{2,1,0:T(8,128)(2,1)} %g_hbm.1, bf16[9,69,256]{2,1,0:T(8,128)(2,1)} %bitcast.8, bf16[9,69,256]{2,1,0:T(8,128)(2,1)} %bitcast.9), custom_call_target="tpu_custom_call" | custom-call | tf_op jit(solution)/shard_map/pallas_call | solution.py:624
  31.6 1.5 %shard_map.76 = (bf16[69,16,128]{2,1,0:T(8,128)(2,1)}, bf16[256,16,128]{2,1,0:T(8,128)(2,1)}, f32[9,69,256]{2,1,0:T(8,128)}, f32[9,69,256]{2,1,0:T(8,128)}) custom-call(bf16[69,16,128]{2,1,0:T(8,128)(2,1)S(1)} %get-tuple-element.11.reb_in, bf16[256,16,128]{2,1,0:T(8,128)(2,1)S(1)} %get-tuple-element.12.feat_in, ...), custom_call_target="tpu_custom_call" | custom-call | tf_op jit(solution)/shard_map/pallas_call | solution.py:676

commit v6 on v5

--- a/solution.py
+++ b/solution.py
@@ -353,6 +353,8 @@
         source = lax.rem(half + (turn if forward else halves - turn), halves)
         return source * inner + lax.rem(row_at + swap, inner)
 
+    leaving = []
+
     def start_pair(stream):
         copies = {}
         for index in list(range(plane - 1, 0, -1)) + [0]:
@@ -366,7 +368,7 @@
     def start_lon(stream, copies):
         onward = {}
         for index in range(plane - 1, 0, -1):
-            copies[index].wait()
+            copies[index].wait_recv()
             for rank in reversed(range(owners)):
                 place = owner(rank) - base
                 chunk = block_of(index, True) * owners + place
@@ -380,7 +382,8 @@
                     from_lon.at[stream, index - 1, place],
                     stream * 6 + 1, slot, slot, plane_peer(index),
                 )
-        copies[0].wait()
+        copies[0].wait_recv()
+        leaving.extend(list(copies.values()) + list(onward.values()))
         return onward
 
     def start_lat(stream, copies):
@@ -390,7 +393,7 @@
             part = piece(block_of(0, True) * owners + place, per)
             total = parts[stream, core, part] + from_pair[stream, part]
             for index in range(plane - 1, 0, -1):
-                copies[index, rank].wait()
+                copies[index, rank].wait_recv()
                 total = total + from_lon[stream, index - 1, place].astype(F32)
             lat_out[stream, place] = total.astype(LINK)
 
@@ -577,6 +580,8 @@
     start_pair_gather(1)
     finish(0)
     finish(1)
+    for copy in leaving:
+        copy.wait_send()
 
 
 def finish_kernel(norm, reb_in, feat_in, grad_in, reb_out, feat_out, enc_out, gen_out, flat, ready, sem):

time: 33.3 us -> 33.3 us (level)
  no operation moved by 1% of the time
where the time goes in v6:
time: 33.3 us; the launch traced here: 33.2 us
  Pallas kernels  32.5 us (98%)
  between operations  0.64 us (2%)
    pallas_call x1, Pallas kernels, on_device(): pl.pallas_call(functools.partial(layer_kernel, lats, halves, deep), out_s...  31 us
    pallas_call x1, Pallas kernels, on_device(): pl.pallas_call(functools.partial(finish_kernel, norm), out_shape=[jax.Sha...  1.53 us

profile of v6, /device:TPU:0, one launch (start us, length us, event | category | flops | bytes accessed | tf_op | source)
XLA Modules:
  0.0 33.2 jit_solution(4799258592608006906)
XLA Ops:
  0.6 31.0 %shard_map.75 = (bf16[69,16,128]{2,1,0:T(8,128)(2,1)S(1)}, bf16[256,16,128]{2,1,0:T(8,128)(2,1)S(1)}, bf16[2,2,8,80,128]{4,3,2,1,0:T(8,128)(2,1)S(1)}) custom-call(bf16[69,16,128]{2,1,0:T(8,128)(2,1)} %f_hbm.1, bf16[69,16,128]{2,1,0:T(8,128)(2,1)} %g_hbm.1, bf16[9,69,256]{2,1,0:T(8,128)(2,1)} %bitcast.8, bf16[9,69,256]{2,1,0:T(8,128)(2,1)} %bitcast.9), custom_call_target="tpu_custom_call" | custom-call | tf_op jit(solution)/shard_map/pallas_call | solution.py:629
  31.6 1.5 %shard_map.76 = (bf16[69,16,128]{2,1,0:T(8,128)(2,1)}, bf16[256,16,128]{2,1,0:T(8,128)(2,1)}, f32[9,69,256]{2,1,0:T(8,128)}, f32[9,69,256]{2,1,0:T(8,128)}) custom-call(bf16[69,16,128]{2,1,0:T(8,128)(2,1)S(1)} %get-tuple-element.11.reb_in, bf16[256,16,128]{2,1,0:T(8,128)(2,1)S(1)} %get-tuple-element.12.feat_in, ...), custom_call_target="tpu_custom_call" | custom-call | tf_op jit(solution)/shard_map/pallas_call | solution.py:681
